TPU v7x, 32 devices: a whole 2x2x4 slice. The times are simulated.
32 devices in a mesh: users: 16 (over z, y, x), rep: 2 (over core).
Axes of the slice: x: 2, y: 2, z: 4, core: 2. Of those that a mesh axis runs over, the one named last changes fastest.
Arguments:
- user_factors: float32 [16384, 256], P('users'), may hold values from -1.5 to 1.5
- user_accum: float32 [16384, 256], P('users'), may hold values from 0.5 to 8
- item_factors: float32 [4096, 256], P('users'), may hold values from -1.5 to 1.5
- item_accum: float32 [4096, 256], P('users'), may hold values from 0.5 to 8
- tile_counts: bfloat16 [16, 2, 128, 128, 128], P('users', 'rep'), may hold values from 0 to 20, as said below
- tile_user: int32 [16, 2, 128], P('users', 'rep'), may hold values from 0 to 7
- tile_item: int32 [16, 2, 128], P('users', 'rep'), may hold values from 0 to 31, as said below
- send_list: int32 [16, 2, 16], P('users', 'rep'), may hold values from 0 to 2, as said below
Outputs:
- new_users: float32 [16384, 256], P('users')
- new_user_accum: float32 [16384, 256], P('users')
- new_items: float32 [4096, 256], P('users')
- new_item_accum: float32 [4096, 256], P('users')
Inputs may be any that keep to these rules, and one draw needn't show every extreme that they name: `tile_counts`: zero means no interaction. `tile_item`: panel b belongs to owner b // 2. Device (q, r) uses at most one panel of each owner o, namely o * 2 + send_list[o, r, q], and only where send_list[o, r, q] < 2. `send_list`: the value 2 means that requester q uses no panel of owner o.
All inputs are finite; a program needn't handle non-finite values.
Results may differ from a plain program's by a relative error of at most 0.0026.
Values may be sent and summed in bfloat16 or wider, within the bound.
No kernel may reach another device: no remote copies, remote signals or barrier semaphores. Data moves between devices by JAX's collectives and lax.ppermute only.
A program may use at most 128 MiB of HBM per device.

v0:
```python
import math
import jax
import jax.numpy as jnp
from jax import lax
from jax.sharding import PartitionSpec as P

CONF_SLOPE = 0.5
ERR_SCALE = 1.0 / 64.0


def tile_terms(user_strip, panels, counts, users_idx, fetch_index, slot_index, slot_count):
    tile_count = counts.shape[0]
    group_size = math.gcd(tile_count, 32)
    group_count = tile_count // group_size
    side = counts.shape[-1]
    width = panels.shape[-1]

    def tile_step(totals, inputs):
        user_total, slot_total = totals
        block_counts, block_user, block_fetch, block_slot = inputs
        user_rows = user_strip[block_user]
        item_rows = panels[block_fetch]
        predicted = jnp.einsum(
            "gur,gir->gui", user_rows, item_rows, preferred_element_type=jnp.float32
        )
        amount = block_counts.astype(jnp.float32)
        confidence = 1.0 + CONF_SLOPE * amount
        preference = jnp.where(amount > 0, 1.0, 0.0).astype(jnp.float32)
        weighted_err = (confidence * (predicted - preference) * ERR_SCALE).astype(jnp.bfloat16)
        user_part = jnp.einsum(
            "gui,gir->gur", weighted_err, item_rows, preferred_element_type=jnp.float32
        )
        item_part = jnp.einsum(
            "gui,gur->gir", weighted_err, user_rows, preferred_element_type=jnp.float32
        )
        user_total = user_total.at[block_user].add(user_part)
        slot_total = slot_total.at[block_slot].add(item_part)
        return ((user_total, slot_total), None)

    start = (
        jnp.zeros((user_strip.shape[0], side, width), jnp.float32),
        jnp.zeros((slot_count, side, width), jnp.float32),
    )
    inputs = (
        counts.reshape(group_count, group_size, side, side),
        users_idx.reshape(group_count, group_size),
        fetch_index.reshape(group_count, group_size),
        slot_index.reshape(group_count, group_size),
    )
    (user_total, slot_total), _ = lax.scan(tile_step, start, inputs)
    return (user_total, slot_total)


def adagrad(factors, accum, grad):
    new_accum = accum + grad * grad
    return (factors - grad / jnp.sqrt(new_accum), new_accum)


def local(
    user_factors, user_accum, item_factors, item_accum, tile_counts, tile_user, tile_item, send_list
):
    tile_size = tile_counts.shape[-1]
    feat_width = user_factors.shape[1]
    user_strip = user_factors.astype(jnp.bfloat16).reshape(-1, tile_size, feat_width)
    owned_panels = item_factors.astype(jnp.bfloat16).reshape(-1, tile_size, feat_width)
    panels_own = owned_panels.shape[0]
    peer_count = lax.axis_size("users")
    counts = tile_counts[0, 0]
    users_idx = tile_user[0, 0]
    items_idx = tile_item[0, 0]
    send_row = send_list[0, 0]
    slot_index = items_idx // panels_own
    outgoing = owned_panels[jnp.minimum(send_row, panels_own - 1)]
    panels = lax.all_to_all(outgoing, "users", split_axis=0, concat_axis=0, tiled=True)
    user_part, slot_part = tile_terms(
        user_strip, panels, counts, users_idx, slot_index, slot_index, peer_count
    )
    returned = lax.all_to_all(
        slot_part.astype(jnp.bfloat16), "users", split_axis=0, concat_axis=0, tiled=True
    )
    selector = (send_row[None, :] == jnp.arange(panels_own, dtype=jnp.int32)[:, None]).astype(
        jnp.bfloat16
    )
    item_part = jnp.einsum("kq,qir->kir", selector, returned, preferred_element_type=jnp.float32)
    item_part = item_part.reshape(-1, feat_width)
    user_grad = lax.psum(user_part.reshape(-1, feat_width), "rep")
    new_users, new_user_accum = adagrad(user_factors, user_accum, user_grad)
    item_grad = lax.psum(item_part, "rep")
    new_items, new_item_accum = adagrad(item_factors, item_accum, item_grad)
    return (new_users, new_user_accum, new_items, new_item_accum)


def solution(mesh):
    return jax.shard_map(
        local,
        mesh=mesh,
        in_specs=(
            P("users", None),
            P("users", None),
            P("users", None),
            P("users", None),
            P("users", "rep", None, None, None),
            P("users", "rep", None),
            P("users", "rep", None),
            P("users", "rep", None),
        ),
        out_specs=(P("users", None), P("users", None), P("users", None), P("users", None)),
        check_vma=False,
    )
```

profile of v0, /device:TPU:0, one launch (start us, length us, event | category | flops | bytes accessed | tf_op | source)
XLA Modules:
  0.0 230.2 jit_solution(15211641022157744401)
XLA Ops:
  7.2 0.7 fusion.16
  7.8 1.0 convert_element_type.20
  8.8 0.0 copy-start.10
  8.8 0.0 copy-start.11
  8.8 0.0 copy-start.4
  8.8 1.6 gather_fusion.2
  10.4 8.3 %all-to-all-start = ((bf16[16,128,256]{2,1,0:T(8,128)(2,1)}), bf16[16,128,256]{2,1,0:T(8,128)(2,1)S(1)}, u32[]{:S(2)}, u32[]{:S(2)}) async-start(bf16[16,128,256]{2,1,0:T(8,128)(2,1)} %gather_fusion.2), calls=%async_computation | async-start | bytes 2097152 | tf_op jit(solution)/shard_map/all_to_all | solution.py:74
  18.8 0.0 all-reduce.3.cloned.1.call-start
  18.8 0.5 broadcast.149
  19.3 0.7 reduce.6
  20.0 0.7 reduce.7
  20.7 0.1 squeeze.18
  20.8 0.1 reshape_squeeze.6
  20.8 0.9 convert_element_type.19
  21.7 21.4 %all-to-all-done = bf16[16,128,256]{2,1,0:T(8,128)(2,1)S(1)} async-done(((bf16[16,128,256]{2,1,0:T(8,128)(2,1)}), bf16[16,128,256]{2,1,0:T(8,128)(2,1)S(1)}, u32[]{:S(2)}, u32[]{:S(2)}) %all-to-all-start) | async-done | bytes 1048608 | tf_op jit(solution)/shard_map/all_to_all | solution.py:74
  43.2 1.0 copy-done.2
  44.1 0.1 broadcast_in_dim.15
  44.2 0.2 broadcast_in_dim.20
  44.4 123.8 %while.13 = (s32[]{:T(128)}, f32[8,128,256]{2,1,0:T(8,128)S(1)}, f32[16,128,256]{2,1,0:T(8,128)S(1)}, s32[4,32]{1,0:T(4,128)S(1)}, bf16[4,32,128,128]{3,2,1,0:T(...) while((s32[]{:T(128)}, f32[8,128,256]{2,1,0:T(8,128)S(1)}, ...), condition=%wide.region_3.4_spmd, body=%wide.region_0.3_spmd.sunk | while | flops 812124352 | bytes 67118496 | solution.py:50
  44.5 3.2 %gather_fusion.1 = bf16[32,128,256]{2,1,0:T(8,128)(2,1)} fusion(bf16[16,128,256]{2,1,0:T(8,128)(2,1)} %get-tuple-element.173, s32[1024]{0:T(1024)S(1)} %pad_clamp_fusion.6), kind=kCustom, calls=%fused_computation.1.clone.1 | custom fusion | bytes 4194432 | tf_op jit(solution)/shard_map/while/body/eval_jaxpr/gather | solution.py:22
  47.7 3.1 %gather_fusion = bf16[32,128,256]{2,1,0:T(8,128)(2,1)} fusion(bf16[8,128,256]{2,1,0:T(8,128)(2,1)} %get-tuple-element.171, s32[1024]{0:T(1024)S(1)} %pad_clamp_fusion.5), kind=kCustom, calls=%fused_computation.clone.1 | custom fusion | bytes 4194432 | tf_op jit(solution)/shard_map/while/body/eval_jaxpr/gather | solution.py:21
  50.8 3.4 %fusion.43 = bf16[32,128,128]{2,1,0:T(8,128)(2,1)S(1)} fusion(bf16[32,128,256]{2,1,0:T(8,128)(2,1)} %gather_fusion, bf16[32,128,256]{2,1,0:T(8,128)(2,1)} %gather_fusion.1, bf16[4,32,128,128]{3,2,1,0:T(8,128)(2,1)} %get-tuple-element.170, s32[]{:T(128)S(6)} %copy.28), kind=kOutput, calls=%fused_computation.11.clone.1 | convolution fusion | flops 273154048 | bytes 6291460 | tf_op jit(solution)/shard_map/while/body/eval_jaxpr/gur,gir->gui/dot_general | solution.py:23
  54.2 0.0 copy-start.3
  54.2 1.0 copy-done.3
  55.2 2.7 %fusion.45 = f32[32,128,256]{2,1,0:T(8,128)} fusion(bf16[32,128,128]{2,1,0:T(8,128)(2,1)S(1)} %fusion.43, bf16[32,128,256]{2,1,0:T(8,128)(2,1)S(1)} %copy-done.1), kind=kOutput, calls=%fused_computation.44.clone.1 | convolution fusion | flops 268435456 | bytes 7340032 | tf_op jit(solution)/shard_map/while/body/eval_jaxpr/gui,gur->gir/dot_general | solution.py:33
  57.9 6.5 %scatter_fusion.1 = f32[16,128,256]{2,1,0:T(8,128)S(1)} fusion(f32[16,128,256]{2,1,0:T(8,128)S(1)} %get-tuple-element.159, s32[32]{0:T(128)S(1)} %get-tuple-element.147, f32[32,128,256]{2,1,0:T(8,128)} %fusion.45), kind=kCustom, calls=%fused_computation.4.clone.1 | custom fusion | flops 1048576 | bytes 12583040 | tf_op jit(solution)/shard_map/while/body/eval_jaxpr/scatter-add | solution.py:37
  64.3 4.6 %fusion.44 = f32[32,128,256]{2,1,0:T(8,128)} fusion(bf16[32,128,128]{2,1,0:T(8,128)(2,1)} %copy-done.3, bf16[32,128,256]{2,1,0:T(8,128)(2,1)} %gather_fusion.1), kind=kOutput, calls=%fused_computation.43.clone.1 | convolution fusion | flops 268435456 | bytes 7340032 | tf_op jit(solution)/shard_map/while/body/eval_jaxpr/gui,gir->gur/dot_general | solution.py:30
  68.9 6.5 %scatter_fusion = f32[8,128,256]{2,1,0:T(8,128)S(1)} fusion(f32[8,128,256]{2,1,0:T(8,128)S(1)} %get-tuple-element.158, s32[32]{0:T(128)S(1)} %get-tuple-element.146, f32[32,128,256]{2,1,0:T(8,128)} %fusion.44), kind=kCustom, calls=%fused_computation.3.clone.1 | custom fusion | flops 1048576 | bytes 12583040 | tf_op jit(solution)/shard_map/while/body/eval_jaxpr/scatter-add | solution.py:36
  75.4 3.2 %gather_fusion.1 = bf16[32,128,256]{2,1,0:T(8,128)(2,1)} fusion(bf16[16,128,256]{2,1,0:T(8,128)(2,1)} %get-tuple-element.173, s32[1024]{0:T(1024)S(1)} %pad_clamp_fusion.6), kind=kCustom, calls=%fused_computation.1.clone.1 | custom fusion | bytes 4194432 | tf_op jit(solution)/shard_map/while/body/eval_jaxpr/gather | solution.py:22
  78.7 3.1 %gather_fusion = bf16[32,128,256]{2,1,0:T(8,128)(2,1)} fusion(bf16[8,128,256]{2,1,0:T(8,128)(2,1)} %get-tuple-element.171, s32[1024]{0:T(1024)S(1)} %pad_clamp_fusion.5), kind=kCustom, calls=%fused_computation.clone.1 | custom fusion | bytes 4194432 | tf_op jit(solution)/shard_map/while/body/eval_jaxpr/gather | solution.py:21
  81.7 3.4 %fusion.43 = bf16[32,128,128]{2,1,0:T(8,128)(2,1)S(1)} fusion(bf16[32,128,256]{2,1,0:T(8,128)(2,1)} %gather_fusion, bf16[32,128,256]{2,1,0:T(8,128)(2,1)} %gather_fusion.1, bf16[4,32,128,128]{3,2,1,0:T(8,128)(2,1)} %get-tuple-element.170, s32[]{:T(128)S(6)} %copy.28), kind=kOutput, calls=%fused_computation.11.clone.1 | convolution fusion | flops 273154048 | bytes 6291460 | tf_op jit(solution)/shard_map/while/body/eval_jaxpr/gur,gir->gui/dot_general | solution.py:23
  85.1 0.0 copy-start.3
  85.1 1.0 copy-done.3
  86.1 2.7 %fusion.45 = f32[32,128,256]{2,1,0:T(8,128)} fusion(bf16[32,128,128]{2,1,0:T(8,128)(2,1)S(1)} %fusion.43, bf16[32,128,256]{2,1,0:T(8,128)(2,1)S(1)} %copy-done.1), kind=kOutput, calls=%fused_computation.44.clone.1 | convolution fusion | flops 268435456 | bytes 7340032 | tf_op jit(solution)/shard_map/while/body/eval_jaxpr/gui,gur->gir/dot_general | solution.py:33
  88.8 6.5 %scatter_fusion.1 = f32[16,128,256]{2,1,0:T(8,128)S(1)} fusion(f32[16,128,256]{2,1,0:T(8,128)S(1)} %get-tuple-element.159, s32[32]{0:T(128)S(1)} %get-tuple-element.147, f32[32,128,256]{2,1,0:T(8,128)} %fusion.45), kind=kCustom, calls=%fused_computation.4.clone.1 | custom fusion | flops 1048576 | bytes 12583040 | tf_op jit(solution)/shard_map/while/body/eval_jaxpr/scatter-add | solution.py:37
  95.3 4.6 %fusion.44 = f32[32,128,256]{2,1,0:T(8,128)} fusion(bf16[32,128,128]{2,1,0:T(8,128)(2,1)} %copy-done.3, bf16[32,128,256]{2,1,0:T(8,128)(2,1)} %gather_fusion.1), kind=kOutput, calls=%fused_computation.43.clone.1 | convolution fusion | flops 268435456 | bytes 7340032 | tf_op jit(solution)/shard_map/while/body/eval_jaxpr/gui,gir->gur/dot_general | solution.py:30
  99.8 6.5 %scatter_fusion = f32[8,128,256]{2,1,0:T(8,128)S(1)} fusion(f32[8,128,256]{2,1,0:T(8,128)S(1)} %get-tuple-element.158, s32[32]{0:T(128)S(1)} %get-tuple-element.146, f32[32,128,256]{2,1,0:T(8,128)} %fusion.44), kind=kCustom, calls=%fused_computation.3.clone.1 | custom fusion | flops 1048576 | bytes 12583040 | tf_op jit(solution)/shard_map/while/body/eval_jaxpr/scatter-add | solution.py:36
  106.4 3.2 %gather_fusion.1 = bf16[32,128,256]{2,1,0:T(8,128)(2,1)} fusion(bf16[16,128,256]{2,1,0:T(8,128)(2,1)} %get-tuple-element.173, s32[1024]{0:T(1024)S(1)} %pad_clamp_fusion.6), kind=kCustom, calls=%fused_computation.1.clone.1 | custom fusion | bytes 4194432 | tf_op jit(solution)/shard_map/while/body/eval_jaxpr/gather | solution.py:22
  109.6 3.1 %gather_fusion = bf16[32,128,256]{2,1,0:T(8,128)(2,1)} fusion(bf16[8,128,256]{2,1,0:T(8,128)(2,1)} %get-tuple-element.171, s32[1024]{0:T(1024)S(1)} %pad_clamp_fusion.5), kind=kCustom, calls=%fused_computation.clone.1 | custom fusion | bytes 4194432 | tf_op jit(solution)/shard_map/while/body/eval_jaxpr/gather | solution.py:21
  112.7 3.4 %fusion.43 = bf16[32,128,128]{2,1,0:T(8,128)(2,1)S(1)} fusion(bf16[32,128,256]{2,1,0:T(8,128)(2,1)} %gather_fusion, bf16[32,128,256]{2,1,0:T(8,128)(2,1)} %gather_fusion.1, bf16[4,32,128,128]{3,2,1,0:T(8,128)(2,1)} %get-tuple-element.170, s32[]{:T(128)S(6)} %copy.28), kind=kOutput, calls=%fused_computation.11.clone.1 | convolution fusion | flops 273154048 | bytes 6291460 | tf_op jit(solution)/shard_map/while/body/eval_jaxpr/gur,gir->gui/dot_general | solution.py:23
  116.1 0.0 copy-start.3
  116.1 1.0 copy-done.3
  117.0 2.7 %fusion.45 = f32[32,128,256]{2,1,0:T(8,128)} fusion(bf16[32,128,128]{2,1,0:T(8,128)(2,1)S(1)} %fusion.43, bf16[32,128,256]{2,1,0:T(8,128)(2,1)S(1)} %copy-done.1), kind=kOutput, calls=%fused_computation.44.clone.1 | convolution fusion | flops 268435456 | bytes 7340032 | tf_op jit(solution)/shard_map/while/body/eval_jaxpr/gui,gur->gir/dot_general | solution.py:33
  119.7 6.5 %scatter_fusion.1 = f32[16,128,256]{2,1,0:T(8,128)S(1)} fusion(f32[16,128,256]{2,1,0:T(8,128)S(1)} %get-tuple-element.159, s32[32]{0:T(128)S(1)} %get-tuple-element.147, f32[32,128,256]{2,1,0:T(8,128)} %fusion.45), kind=kCustom, calls=%fused_computation.4.clone.1 | custom fusion | flops 1048576 | bytes 12583040 | tf_op jit(solution)/shard_map/while/body/eval_jaxpr/scatter-add | solution.py:37
  126.2 4.5 %fusion.44 = f32[32,128,256]{2,1,0:T(8,128)} fusion(bf16[32,128,128]{2,1,0:T(8,128)(2,1)} %copy-done.3, bf16[32,128,256]{2,1,0:T(8,128)(2,1)} %gather_fusion.1), kind=kOutput, calls=%fused_computation.43.clone.1 | convolution fusion | flops 268435456 | bytes 7340032 | tf_op jit(solution)/shard_map/while/body/eval_jaxpr/gui,gir->gur/dot_general | solution.py:30
  130.8 6.5 %scatter_fusion = f32[8,128,256]{2,1,0:T(8,128)S(1)} fusion(f32[8,128,256]{2,1,0:T(8,128)S(1)} %get-tuple-element.158, s32[32]{0:T(128)S(1)} %get-tuple-element.146, f32[32,128,256]{2,1,0:T(8,128)} %fusion.44), kind=kCustom, calls=%fused_computation.3.clone.1 | custom fusion | flops 1048576 | bytes 12583040 | tf_op jit(solution)/shard_map/while/body/eval_jaxpr/scatter-add | solution.py:36
  137.3 3.2 %gather_fusion.1 = bf16[32,128,256]{2,1,0:T(8,128)(2,1)} fusion(bf16[16,128,256]{2,1,0:T(8,128)(2,1)} %get-tuple-element.173, s32[1024]{0:T(1024)S(1)} %pad_clamp_fusion.6), kind=kCustom, calls=%fused_computation.1.clone.1 | custom fusion | bytes 4194432 | tf_op jit(solution)/shard_map/while/body/eval_jaxpr/gather | solution.py:22
  140.5 3.1 %gather_fusion = bf16[32,128,256]{2,1,0:T(8,128)(2,1)} fusion(bf16[8,128,256]{2,1,0:T(8,128)(2,1)} %get-tuple-element.171, s32[1024]{0:T(1024)S(1)} %pad_clamp_fusion.5), kind=kCustom, calls=%fused_computation.clone.1 | custom fusion | bytes 4194432 | tf_op jit(solution)/shard_map/while/body/eval_jaxpr/gather | solution.py:21
  143.6 3.4 %fusion.43 = bf16[32,128,128]{2,1,0:T(8,128)(2,1)S(1)} fusion(bf16[32,128,256]{2,1,0:T(8,128)(2,1)} %gather_fusion, bf16[32,128,256]{2,1,0:T(8,128)(2,1)} %gather_fusion.1, bf16[4,32,128,128]{3,2,1,0:T(8,128)(2,1)} %get-tuple-element.170, s32[]{:T(128)S(6)} %copy.28), kind=kOutput, calls=%fused_computation.11.clone.1 | convolution fusion | flops 273154048 | bytes 6291460 | tf_op jit(solution)/shard_map/while/body/eval_jaxpr/gur,gir->gui/dot_general | solution.py:23
  147.0 0.0 copy-start.3
  147.0 1.0 copy-done.3
  148.0 2.7 %fusion.45 = f32[32,128,256]{2,1,0:T(8,128)} fusion(bf16[32,128,128]{2,1,0:T(8,128)(2,1)S(1)} %fusion.43, bf16[32,128,256]{2,1,0:T(8,128)(2,1)S(1)} %copy-done.1), kind=kOutput, calls=%fused_computation.44.clone.1 | convolution fusion | flops 268435456 | bytes 7340032 | tf_op jit(solution)/shard_map/while/body/eval_jaxpr/gui,gur->gir/dot_general | solution.py:33
  150.7 6.5 %scatter_fusion.1 = f32[16,128,256]{2,1,0:T(8,128)S(1)} fusion(f32[16,128,256]{2,1,0:T(8,128)S(1)} %get-tuple-element.159, s32[32]{0:T(128)S(1)} %get-tuple-element.147, f32[32,128,256]{2,1,0:T(8,128)} %fusion.45), kind=kCustom, calls=%fused_computation.4.clone.1 | custom fusion | flops 1048576 | bytes 12583040 | tf_op jit(solution)/shard_map/while/body/eval_jaxpr/scatter-add | solution.py:37
  157.2 4.6 %fusion.44 = f32[32,128,256]{2,1,0:T(8,128)} fusion(bf16[32,128,128]{2,1,0:T(8,128)(2,1)} %copy-done.3, bf16[32,128,256]{2,1,0:T(8,128)(2,1)} %gather_fusion.1), kind=kOutput, calls=%fused_computation.43.clone.1 | convolution fusion | flops 268435456 | bytes 7340032 | tf_op jit(solution)/shard_map/while/body/eval_jaxpr/gui,gir->gur/dot_general | solution.py:30
  161.7 6.5 %scatter_fusion = f32[8,128,256]{2,1,0:T(8,128)S(1)} fusion(f32[8,128,256]{2,1,0:T(8,128)S(1)} %get-tuple-element.158, s32[32]{0:T(128)S(1)} %get-tuple-element.146, f32[32,128,256]{2,1,0:T(8,128)} %fusion.44), kind=kCustom, calls=%fused_computation.3.clone.1 | custom fusion | flops 1048576 | bytes 12583040 | tf_op jit(solution)/shard_map/while/body/eval_jaxpr/scatter-add | solution.py:36
  168.2 0.1 convert_element_type.21
  168.4 30.6 %all_to_all.10 = bf16[16,128,256]{2,1,0:T(8,128)(2,1)S(1)} all-to-all(bf16[16,128,256]{2,1,0:T(8,128)(2,1)S(1)} %convert_element_type.21), channel_id=1, replica_groups=mesh['users'=16,'rep'=2] {'users'}, dimensions={0} | all-to-all | bytes 2097152 | tf_op jit(solution)/shard_map/all_to_all | solution.py:78
  199.0 0.0 copy-start.6
  199.0 0.7 fusion.9
  199.7 0.7 copy.19
  200.4 0.0 all-reduce.3.cloned.1.call-update
  200.4 18.4 %all-reduce.3.cloned.1.call-done = (f32[1024,256]{1,0:T(8,128)}, f32[256,256]{1,0:T(8,128)}) async-done(((f32[1024,256]{1,0:T(8,128)}, f32[256,256]{1,0:T(8,128)}), (f32[1024,256]{1,0:T(8,128)}, f32[256,256]{1,0:T(8,128)})) %all-reduce.3.cloned.1.call-update) | async-done | bytes 1310736 | tf_op jit(solution)/shard_map/psum | solution.py:86
  218.8 1.8 multiply_subtract_fusion.1
  220.6 2.7 %multiply_subtract_fusion = (f32[1024,256]{1,0:T(8,128)}, f32[1024,256]{1,0:T(8,128)}) fusion(f32[1024,256]{1,0:T(8,128)S(1)} %copy-done.5, f32[1024,256]{1,0:T(8,128)} %get-tuple-element.87, f32[1024,256]{1,0:T(8,128)S(1)} %copy-done.6), kind=kLoop, calls=%fused_computation.25 | loop fusion | flops 1048576 | bytes 5242880 | tf_op jit(solution)/shard_map/sub | solution.py:56
  (37 shorter events, 0.2 us)
Async XLA Ops:
  8.8 10.5 %copy-start.10 = (s32[1,1,128]{2,1,0:T(1,128)S(1)}, s32[1,1,128]{2,1,0:T(1,128)}, u32[]{:S(2)}) copy-start(s32[1,1,128]{2,1,0:T(1,128)} %param.15) | copy-start | bytes 1540
  8.8 11.2 %copy-start.11 = (s32[1,1,128]{2,1,0:T(1,128)S(1)}, s32[1,1,128]{2,1,0:T(1,128)}, u32[]{:S(2)}) copy-start(s32[1,1,128]{2,1,0:T(1,128)} %param.16) | copy-start | bytes 1540
  8.8 12.0 %copy-start.4 = (f32[1024,256]{1,0:T(8,128)S(1)}, f32[1024,256]{1,0:T(8,128)}, u32[]{:S(2)}) copy-start(f32[1024,256]{1,0:T(8,128)} %param.10) | copy-start | bytes 3145732
  10.4 32.7 %all-to-all-start = ((bf16[16,128,256]{2,1,0:T(8,128)(2,1)}), bf16[16,128,256]{2,1,0:T(8,128)(2,1)S(1)}, u32[]{:S(2)}, u32[]{:S(2)}) async-start(bf16[16,128,256]{2,1,0:T(8,128)(2,1)} %gather_fusion.2), calls=%async_computation | async-start | bytes 2097152 | tf_op jit(solution)/shard_map/all_to_all | solution.py:74
  18.8 200.0 %all-reduce.3.cloned.1.call-start = ((), (), s32[]{:S(2)}) async-start(), calls=%async_computation.2 | async-start | bytes 2621440 | tf_op jit(solution)/shard_map/psum | solution.py:86
  43.2 1.0 copy-start.2
  50.8 4.4 %copy-start.1 = (bf16[32,128,256]{2,1,0:T(8,128)(2,1)S(1)}, bf16[32,128,256]{2,1,0:T(8,128)(2,1)}, u32[]{:S(2)}) copy-start(bf16[32,128,256]{2,1,0:T(8,128)(2,1)} %gather_fusion) | copy-start | bytes 6291460 | tf_op jit(solution)/shard_map/while
  54.2 1.0 copy-start.3
  81.7 4.4 %copy-start.1 = (bf16[32,128,256]{2,1,0:T(8,128)(2,1)S(1)}, bf16[32,128,256]{2,1,0:T(8,128)(2,1)}, u32[]{:S(2)}) copy-start(bf16[32,128,256]{2,1,0:T(8,128)(2,1)} %gather_fusion) | copy-start | bytes 6291460 | tf_op jit(solution)/shard_map/while
  85.1 1.0 copy-start.3
  112.7 4.4 %copy-start.1 = (bf16[32,128,256]{2,1,0:T(8,128)(2,1)S(1)}, bf16[32,128,256]{2,1,0:T(8,128)(2,1)}, u32[]{:S(2)}) copy-start(bf16[32,128,256]{2,1,0:T(8,128)(2,1)} %gather_fusion) | copy-start | bytes 6291460 | tf_op jit(solution)/shard_map/while
  116.1 1.0 copy-start.3
  143.6 4.4 %copy-start.1 = (bf16[32,128,256]{2,1,0:T(8,128)(2,1)S(1)}, bf16[32,128,256]{2,1,0:T(8,128)(2,1)}, u32[]{:S(2)}) copy-start(bf16[32,128,256]{2,1,0:T(8,128)(2,1)} %gather_fusion) | copy-start | bytes 6291460 | tf_op jit(solution)/shard_map/while
  147.0 1.0 copy-start.3
  168.2 30.8 %copy-start = (f32[8,128,256]{2,1,0:T(8,128)}, f32[8,128,256]{2,1,0:T(8,128)S(1)}, u32[]{:S(2)}) copy-start(f32[8,128,256]{2,1,0:T(8,128)S(1)} %get-tuple-element.69) | copy-start | bytes 3145732
  168.2 30.8 %copy-start.9 = (s32[1,1,16]{2,1,0:T(1,128)S(1)}, s32[1,1,16]{2,1,0:T(1,128)}, u32[]{:S(2)}) copy-start(s32[1,1,16]{2,1,0:T(1,128)} %param.17) | copy-start | bytes 196
  199.0 19.9 %copy-start.7 = (f32[256,256]{1,0:T(8,128)S(1)}, f32[256,256]{1,0:T(8,128)}, u32[]{:S(2)}) copy-start(f32[256,256]{1,0:T(8,128)} %param.12) | copy-start | bytes 786436
  199.0 19.9 %copy-start.8 = (f32[256,256]{1,0:T(8,128)S(1)}, f32[256,256]{1,0:T(8,128)}, u32[]{:S(2)}) copy-start(f32[256,256]{1,0:T(8,128)} %param.13) | copy-start | bytes 786436
  199.0 21.6 %copy-start.5 = (f32[1024,256]{1,0:T(8,128)S(1)}, f32[1024,256]{1,0:T(8,128)}, u32[]{:S(2)}) copy-start(f32[1024,256]{1,0:T(8,128)} %param.10) | copy-start | bytes 3145732
  199.0 21.6 %copy-start.6 = (f32[1024,256]{1,0:T(8,128)S(1)}, f32[1024,256]{1,0:T(8,128)}, u32[]{:S(2)}) copy-start(f32[1024,256]{1,0:T(8,128)} %param.11) | copy-start | bytes 3145732
Sparse Core Ops, SparseCore 0:
  200.5 18.2 all-reduce.2
where the time goes:
time: 231 us; the launch traced here: 230 us
  other arithmetic  60.3 us (26%)
  matrix products  43.3 us (19%)
  waiting for transfers between devices  39.9 us (17%)
  local copies, waits for them, and re-layouts  33.3 us (14%)
  blocking collectives  30.6 us (13%)
  between operations  14.1 us (6%)
  starting transfers between devices  8.38 us (4%)
    all_to_all x1, blocking collectives, local(): lax.all_to_all(slot_part.astype(jnp.bfloat16), 'users', split_axis=0, con...  30.6 us
    scatter-add x4, other arithmetic, tile_step(): slot_total = slot_total.at[block_slot].add(item_part)  25.9 us
    scatter-add x4, other arithmetic, tile_step(): user_total = user_total.at[block_user].add(user_part)  25.8 us
    all_to_all x1, waiting for transfers between devices, local(): lax.all_to_all(outgoing, 'users', split_axis=0, concat_axis=0, tiled=True)  21.4 us
    psum x1, waiting for transfers between devices, local(): user_grad = lax.psum(user_part.reshape(-1, feat_width), 'rep')  18.4 us
    dot_general x4, matrix products, tile_step(): jnp.einsum('gui,gir->gur', weighted_err, item_rows, preferred_element_typ...  18.2 us
    dot_general x4, matrix products, tile_step(): jnp.einsum('gur,gir->gui', user_rows, item_rows, preferred_element_type=j...  13.6 us
    gather x4, local copies, waits for them, and re-layouts, tile_step(): item_rows = panels[block_fetch]  12.9 us
  transfers between devices with their start and end apart: 2, of which 2 were waited for; matrix products, arithmetic and copies ran while one was open for 1% of the time, Pallas kernels for 0%

commit v1 on v0

--- a/solution.py
+++ b/solution.py
@@ -71,7 +71,18 @@
     send_row = send_list[0, 0]
     slot_index = items_idx // panels_own
     outgoing = owned_panels[jnp.minimum(send_row, panels_own - 1)]
-    panels = lax.all_to_all(outgoing, "users", split_axis=0, concat_axis=0, tiled=True)
+    ways, here = (lax.axis_size("users"), lax.axis_index("users"))
+    width_2 = outgoing.shape[0] // ways
+    shape = list(outgoing.shape)
+    shape[0] = width_2
+    height = shape[0]
+    shape[0] = height * ways
+    panels = jnp.zeros(shape, outgoing.dtype)
+    for mask in range(ways):
+        part = lax.dynamic_slice_in_dim(outgoing, (here ^ mask) * width_2, width_2, axis=0)
+        if mask:
+            part = lax.ppermute(part, "users", [(d, d ^ mask) for d in range(ways)])
+        panels = lax.dynamic_update_slice_in_dim(panels, part, (here ^ mask) * height, axis=0)
     user_part, slot_part = tile_terms(
         user_strip, panels, counts, users_idx, slot_index, slot_index, peer_count
     )

time: 231 us -> 264 us (1.14)
  starting transfers between devices: 8.38 us -> 32.3 us
  waiting for transfers between devices: 39.9 us -> 54.8 us
  blocking collectives: 30.6 us -> 24.1 us
    ppermute x0 -> x15, waiting for transfers between devices: none -> 36.4 us  [local(): part = lax.ppermute(part, 'users', [(d, d ^ mask) for d in range(ways)])]
    ppermute x0 -> x15, starting transfers between devices: none -> 32.2 us  [local(): part = lax.ppermute(part, 'users', [(d, d ^ mask) for d in range(ways)])]
    all_to_all x1 -> x0, waiting for transfers between devices: 21.4 us -> none  [local(): lax.all_to_all(outgoing, 'users', split_axis=0, concat_axis=0, tiled=True)]
    all_to_all x1 -> x0, starting transfers between devices: 8.34 us -> none  [local(): lax.all_to_all(outgoing, 'users', split_axis=0, concat_axis=0, tiled=True)]
    all_to_all x1, blocking collectives: 30.6 us -> 24.1 us  [local(): lax.all_to_all(slot_part.astype(jnp.bfloat16), 'users', split_axis=0, con...]
  transfers between devices with their start and end apart: 2 -> 16, of which waited for: 2 -> 12; matrix products, arithmetic and copies ran while one was open for 1% -> 1% of each run, Pallas kernels for 0% -> 0%
where the time goes in v1:
time: 264 us; the launch traced here: 263 us
  other arithmetic  60.1 us (23%)
  waiting for transfers between devices  54.8 us (21%)
  matrix products  43.3 us (16%)
  local copies, waits for them, and re-layouts  33.5 us (13%)
  starting transfers between devices  32.3 us (12%)
  blocking collectives  24.1 us (9%)
  between operations  14.4 us (5%)
    ppermute x15, waiting for transfers between devices, local(): part = lax.ppermute(part, 'users', [(d, d ^ mask) for d in range(ways)])  36.4 us
    ppermute x15, starting transfers between devices, local(): part = lax.ppermute(part, 'users', [(d, d ^ mask) for d in range(ways)])  32.2 us
    scatter-add x4, other arithmetic, tile_step(): slot_total = slot_total.at[block_slot].add(item_part)  25.9 us
    scatter-add x4, other arithmetic, tile_step(): user_total = user_total.at[block_user].add(user_part)  25.8 us
    all_to_all x1, blocking collectives, local(): lax.all_to_all(slot_part.astype(jnp.bfloat16), 'users', split_axis=0, con...  24.1 us
    psum x1, waiting for transfers between devices, local(): user_grad = lax.psum(user_part.reshape(-1, feat_width), 'rep')  18.4 us
    dot_general x4, matrix products, tile_step(): jnp.einsum('gui,gir->gur', weighted_err, item_rows, preferred_element_typ...  18.2 us
    dot_general x4, matrix products, tile_step(): jnp.einsum('gur,gir->gui', user_rows, item_rows, preferred_element_type=j...  13.6 us
  transfers between devices with their start and end apart: 16, of which 12 were waited for; matrix products, arithmetic and copies ran while one was open for 1% of the time, Pallas kernels for 0%

profile of v1, /device:TPU:0, one launch (start us, length us, event | category | flops | bytes accessed | tf_op | source)
XLA Modules:
  0.0 262.9 jit_solution(4171380172794351859)
XLA Ops:
  7.9 1.0 convert_element_type.20
  9.8 0.9 constant_dynamic-slice_fusion.2
  10.7 7.0 %collective-permute-start.14 = (bf16[1,128,256]{2,1,0:T(8,128)(2,1)S(1)}, bf16[1,128,256]{2,1,0:T(8,128)(2,1)S(1)}, u32[]{:S(2)}, u32[]{:S(2)}) collective-permute-start(bf16[1,128,256]{2,1,0:T(8,128)(2,1)S(1)} %get-tuple-element.95), channel_id=1, source_target_pairs={{0,30},{2,28},{4,26},{6,24},{8,22},{10,20},{12,18},{14,16},{16,14}... | collective-permute-start | bytes 196616 | tf_op jit(solution)/shard_map/ppermute | solution.py:84
  17.8 3.6 %collective-permute-start.12 = (bf16[1,128,256]{2,1,0:T(8,128)(2,1)S(1)}, bf16[1,128,256]{2,1,0:T(8,128)(2,1)S(1)}, u32[]{:S(2)}, u32[]{:S(2)}) collective-permute-start(bf16[1,128,256]{2,1,0:T(8,128)(2,1)S(1)} %get-tuple-element.97), channel_id=1, source_target_pairs={{0,26},{2,24},{4,30},{6,28},{8,18},{10,16},{12,22},{14,20},{16,10}... | collective-permute-start | bytes 196616 | tf_op jit(solution)/shard_map/ppermute | solution.py:84
  21.6 1.6 collective-permute-start
  24.9 0.9 convert_element_type.19
  26.1 1.6 collective-permute-start.1
  27.6 2.9 %collective-permute-done.1 = bf16[1,128,256]{2,1,0:T(8,128)(2,1)S(1)} collective-permute-done((bf16[1,128,256]{2,1,0:T(8,128)(2,1)}, bf16[1,128,256]{2,1,0:T(8,128)(2,1)S(1)}, u32[]{:S(2)}, u32[]{:S(2)}) %collective-permute-start.1) | collective-permute-done | bytes 65568 | tf_op jit(solution)/shard_map/ppermute | solution.py:84
  30.5 2.5 collective-permute-start.2
  33.1 2.9 %collective-permute-done.2 = bf16[1,128,256]{2,1,0:T(8,128)(2,1)S(1)} collective-permute-done((bf16[1,128,256]{2,1,0:T(8,128)(2,1)}, bf16[1,128,256]{2,1,0:T(8,128)(2,1)S(1)}, u32[]{:S(2)}, u32[]{:S(2)}) %collective-permute-start.2) | collective-permute-done | bytes 65568 | tf_op jit(solution)/shard_map/ppermute | solution.py:84
  35.9 4.9 %collective-permute-done.3 = bf16[1,128,256]{2,1,0:T(8,128)(2,1)S(1)} collective-permute-done((bf16[1,128,256]{2,1,0:T(8,128)(2,1)}, bf16[1,128,256]{2,1,0:T(8,128)(2,1)S(1)}, u32[]{:S(2)}, u32[]{:S(2)}) %collective-permute-start.3) | collective-permute-done | bytes 65568 | tf_op jit(solution)/shard_map/ppermute | solution.py:84
  41.4 4.8 %collective-permute-done.4 = bf16[1,128,256]{2,1,0:T(8,128)(2,1)S(1)} collective-permute-done((bf16[1,128,256]{2,1,0:T(8,128)(2,1)}, bf16[1,128,256]{2,1,0:T(8,128)(2,1)S(1)}, u32[]{:S(2)}, u32[]{:S(2)}) %collective-permute-start.4) | collective-permute-done | bytes 65568 | tf_op jit(solution)/shard_map/ppermute | solution.py:84
  46.2 0.9 collective-permute-start.5
  47.2 4.2 %collective-permute-done.5 = bf16[1,128,256]{2,1,0:T(8,128)(2,1)S(1)} collective-permute-done((bf16[1,128,256]{2,1,0:T(8,128)(2,1)S(1)}, bf16[1,128,256]{2,1,0:T(8,128)(2,1)S(1)}, u32[]{:S(2)}, u32[]{:S(2)}) %collective-permute-start.5) | collective-permute-done | bytes 65568 | tf_op jit(solution)/shard_map/ppermute | solution.py:84
  51.4 1.5 collective-permute-start.6
  52.9 4.5 %collective-permute-done.6 = bf16[1,128,256]{2,1,0:T(8,128)(2,1)S(1)} collective-permute-done((bf16[1,128,256]{2,1,0:T(8,128)(2,1)S(1)}, bf16[1,128,256]{2,1,0:T(8,128)(2,1)S(1)}, u32[]{:S(2)}, u32[]{:S(2)}) %collective-permute-start.6) | collective-permute-done | bytes 65568 | tf_op jit(solution)/shard_map/ppermute | solution.py:84
  57.4 2.4 collective-permute-start.7
  59.9 2.7 %collective-permute-done.7 = bf16[1,128,256]{2,1,0:T(8,128)(2,1)S(1)} collective-permute-done((bf16[1,128,256]{2,1,0:T(8,128)(2,1)S(1)}, bf16[1,128,256]{2,1,0:T(8,128)(2,1)S(1)}, u32[]{:S(2)}, u32[]{:S(2)}) %collective-permute-start.7) | collective-permute-done | bytes 65568 | tf_op jit(solution)/shard_map/ppermute | solution.py:84
  62.6 2.8 %collective-permute-start.8 = (bf16[1,128,256]{2,1,0:T(8,128)(2,1)S(1)}, bf16[1,128,256]{2,1,0:T(8,128)(2,1)S(1)}, u32[]{:S(2)}, u32[]{:S(2)}) collective-permute-start(bf16[1,128,256]{2,1,0:T(8,128)(2,1)S(1)} %copy-done.9), channel_id=1, source_target_pairs={{0,18},{2,16},{4,22},{6,20},{8,26},{10,24},{12,30},{14,28},{16,2},... | collective-permute-start | bytes 196616 | tf_op jit(solution)/shard_map/ppermute | solution.py:84
  65.4 3.3 %collective-permute-done.8 = bf16[1,128,256]{2,1,0:T(8,128)(2,1)S(1)} collective-permute-done((bf16[1,128,256]{2,1,0:T(8,128)(2,1)S(1)}, bf16[1,128,256]{2,1,0:T(8,128)(2,1)S(1)}, u32[]{:S(2)}, u32[]{:S(2)}) %collective-permute-start.8) | collective-permute-done | bytes 65568 | tf_op jit(solution)/shard_map/ppermute | solution.py:84
  68.7 4.2 %collective-permute-start.9 = (bf16[1,128,256]{2,1,0:T(8,128)(2,1)S(1)}, bf16[1,128,256]{2,1,0:T(8,128)(2,1)S(1)}, u32[]{:S(2)}, u32[]{:S(2)}) collective-permute-start(bf16[1,128,256]{2,1,0:T(8,128)(2,1)S(1)} %get-tuple-element.100), channel_id=1, source_target_pairs={{0,20},{2,22},{4,16},{6,18},{8,28},{10,30},{12,24},{14,26},{16,4},... | collective-permute-start | bytes 196616 | tf_op jit(solution)/shard_map/ppermute | solution.py:84
  72.9 2.2 collective-permute-done.9
  75.1 3.3 %collective-permute-start.10 = (bf16[1,128,256]{2,1,0:T(8,128)(2,1)S(1)}, bf16[1,128,256]{2,1,0:T(8,128)(2,1)S(1)}, u32[]{:S(2)}, u32[]{:S(2)}) collective-permute-start(bf16[1,128,256]{2,1,0:T(8,128)(2,1)S(1)} %get-tuple-element.99), channel_id=1, source_target_pairs={{0,22},{2,20},{4,18},{6,16},{8,30},{10,28},{12,26},{14,24},{16,6},... | collective-permute-start | bytes 196616 | tf_op jit(solution)/shard_map/ppermute | solution.py:84
  78.4 3.7 %collective-permute-done.10 = bf16[1,128,256]{2,1,0:T(8,128)(2,1)S(1)} collective-permute-done((bf16[1,128,256]{2,1,0:T(8,128)(2,1)S(1)}, bf16[1,128,256]{2,1,0:T(8,128)(2,1)S(1)}, u32[]{:S(2)}, u32[]{:S(2)}) %collective-permute-start.10) | collective-permute-done | bytes 65568 | tf_op jit(solution)/shard_map/ppermute | solution.py:84
  82.2 1.0 copy-done.2
  83.5 123.9 %while.13 = (s32[]{:T(128)}, f32[8,128,256]{2,1,0:T(8,128)S(1)}, f32[16,128,256]{2,1,0:T(8,128)S(1)}, s32[4,32]{1,0:T(4,128)S(1)}, bf16[4,32,128,128]{3,2,1,0:T(...) while((s32[]{:T(128)}, f32[8,128,256]{2,1,0:T(8,128)S(1)}, ...), condition=%wide.region_3.4_spmd, body=%wide.region_0.3_spmd.sunk | while | flops 812124352 | bytes 67118496 | solution.py:50
  83.5 3.3 %gather_fusion.1 = bf16[32,128,256]{2,1,0:T(8,128)(2,1)} fusion(bf16[16,128,256]{2,1,0:T(8,128)(2,1)} %get-tuple-element.189, s32[1024]{0:T(1024)S(1)} %pad_clamp_fusion.6), kind=kCustom, calls=%fused_computation.1.clone.1 | custom fusion | bytes 4194432 | tf_op jit(solution)/shard_map/while/body/eval_jaxpr/gather | solution.py:22
  86.8 3.0 %gather_fusion = bf16[32,128,256]{2,1,0:T(8,128)(2,1)} fusion(bf16[8,128,256]{2,1,0:T(8,128)(2,1)} %get-tuple-element.187, s32[1024]{0:T(1024)S(1)} %pad_clamp_fusion.5), kind=kCustom, calls=%fused_computation.clone.1 | custom fusion | bytes 4194432 | tf_op jit(solution)/shard_map/while/body/eval_jaxpr/gather | solution.py:21
  89.8 3.4 %fusion.43 = bf16[32,128,128]{2,1,0:T(8,128)(2,1)S(1)} fusion(bf16[32,128,256]{2,1,0:T(8,128)(2,1)} %gather_fusion, bf16[32,128,256]{2,1,0:T(8,128)(2,1)} %gather_fusion.1, bf16[4,32,128,128]{3,2,1,0:T(8,128)(2,1)} %get-tuple-element.186, s32[]{:T(128)S(6)} %copy.44), kind=kOutput, calls=%fused_computation.11.clone.1 | convolution fusion | flops 273154048 | bytes 6291460 | tf_op jit(solution)/shard_map/while/body/eval_jaxpr/gur,gir->gui/dot_general | solution.py:23
  93.3 1.0 copy-done.3
  94.2 2.7 %fusion.45 = f32[32,128,256]{2,1,0:T(8,128)} fusion(bf16[32,128,128]{2,1,0:T(8,128)(2,1)S(1)} %fusion.43, bf16[32,128,256]{2,1,0:T(8,128)(2,1)S(1)} %copy-done.1), kind=kOutput, calls=%fused_computation.75.clone.1 | convolution fusion | flops 268435456 | bytes 7340032 | tf_op jit(solution)/shard_map/while/body/eval_jaxpr/gui,gur->gir/dot_general | solution.py:33
  96.9 6.5 %scatter_fusion.1 = f32[16,128,256]{2,1,0:T(8,128)S(1)} fusion(f32[16,128,256]{2,1,0:T(8,128)S(1)} %get-tuple-element.175, s32[32]{0:T(128)S(1)} %get-tuple-element.163, f32[32,128,256]{2,1,0:T(8,128)} %fusion.45), kind=kCustom, calls=%fused_computation.4.clone.1 | custom fusion | flops 1048576 | bytes 12583040 | tf_op jit(solution)/shard_map/while/body/eval_jaxpr/scatter-add | solution.py:37
  103.4 4.6 %fusion.44 = f32[32,128,256]{2,1,0:T(8,128)} fusion(bf16[32,128,128]{2,1,0:T(8,128)(2,1)} %copy-done.3, bf16[32,128,256]{2,1,0:T(8,128)(2,1)} %gather_fusion.1), kind=kOutput, calls=%fused_computation.74.clone.1 | convolution fusion | flops 268435456 | bytes 7340032 | tf_op jit(solution)/shard_map/while/body/eval_jaxpr/gui,gir->gur/dot_general | solution.py:30
  108.0 6.5 %scatter_fusion = f32[8,128,256]{2,1,0:T(8,128)S(1)} fusion(f32[8,128,256]{2,1,0:T(8,128)S(1)} %get-tuple-element.174, s32[32]{0:T(128)S(1)} %get-tuple-element.162, f32[32,128,256]{2,1,0:T(8,128)} %fusion.44), kind=kCustom, calls=%fused_computation.3.clone.1 | custom fusion | flops 1048576 | bytes 12583040 | tf_op jit(solution)/shard_map/while/body/eval_jaxpr/scatter-add | solution.py:36
  114.5 3.3 %gather_fusion.1 = bf16[32,128,256]{2,1,0:T(8,128)(2,1)} fusion(bf16[16,128,256]{2,1,0:T(8,128)(2,1)} %get-tuple-element.189, s32[1024]{0:T(1024)S(1)} %pad_clamp_fusion.6), kind=kCustom, calls=%fused_computation.1.clone.1 | custom fusion | bytes 4194432 | tf_op jit(solution)/shard_map/while/body/eval_jaxpr/gather | solution.py:22
  117.8 3.0 %gather_fusion = bf16[32,128,256]{2,1,0:T(8,128)(2,1)} fusion(bf16[8,128,256]{2,1,0:T(8,128)(2,1)} %get-tuple-element.187, s32[1024]{0:T(1024)S(1)} %pad_clamp_fusion.5), kind=kCustom, calls=%fused_computation.clone.1 | custom fusion | bytes 4194432 | tf_op jit(solution)/shard_map/while/body/eval_jaxpr/gather | solution.py:21
  120.8 3.4 %fusion.43 = bf16[32,128,128]{2,1,0:T(8,128)(2,1)S(1)} fusion(bf16[32,128,256]{2,1,0:T(8,128)(2,1)} %gather_fusion, bf16[32,128,256]{2,1,0:T(8,128)(2,1)} %gather_fusion.1, bf16[4,32,128,128]{3,2,1,0:T(8,128)(2,1)} %get-tuple-element.186, s32[]{:T(128)S(6)} %copy.44), kind=kOutput, calls=%fused_computation.11.clone.1 | convolution fusion | flops 273154048 | bytes 6291460 | tf_op jit(solution)/shard_map/while/body/eval_jaxpr/gur,gir->gui/dot_general | solution.py:23
  124.2 1.0 copy-done.3
  125.2 2.7 %fusion.45 = f32[32,128,256]{2,1,0:T(8,128)} fusion(bf16[32,128,128]{2,1,0:T(8,128)(2,1)S(1)} %fusion.43, bf16[32,128,256]{2,1,0:T(8,128)(2,1)S(1)} %copy-done.1), kind=kOutput, calls=%fused_computation.75.clone.1 | convolution fusion | flops 268435456 | bytes 7340032 | tf_op jit(solution)/shard_map/while/body/eval_jaxpr/gui,gur->gir/dot_general | solution.py:33
  127.9 6.5 %scatter_fusion.1 = f32[16,128,256]{2,1,0:T(8,128)S(1)} fusion(f32[16,128,256]{2,1,0:T(8,128)S(1)} %get-tuple-element.175, s32[32]{0:T(128)S(1)} %get-tuple-element.163, f32[32,128,256]{2,1,0:T(8,128)} %fusion.45), kind=kCustom, calls=%fused_computation.4.clone.1 | custom fusion | flops 1048576 | bytes 12583040 | tf_op jit(solution)/shard_map/while/body/eval_jaxpr/scatter-add | solution.py:37
  134.4 4.6 %fusion.44 = f32[32,128,256]{2,1,0:T(8,128)} fusion(bf16[32,128,128]{2,1,0:T(8,128)(2,1)} %copy-done.3, bf16[32,128,256]{2,1,0:T(8,128)(2,1)} %gather_fusion.1), kind=kOutput, calls=%fused_computation.74.clone.1 | convolution fusion | flops 268435456 | bytes 7340032 | tf_op jit(solution)/shard_map/while/body/eval_jaxpr/gui,gir->gur/dot_general | solution.py:30
  138.9 6.5 %scatter_fusion = f32[8,128,256]{2,1,0:T(8,128)S(1)} fusion(f32[8,128,256]{2,1,0:T(8,128)S(1)} %get-tuple-element.174, s32[32]{0:T(128)S(1)} %get-tuple-element.162, f32[32,128,256]{2,1,0:T(8,128)} %fusion.44), kind=kCustom, calls=%fused_computation.3.clone.1 | custom fusion | flops 1048576 | bytes 12583040 | tf_op jit(solution)/shard_map/while/body/eval_jaxpr/scatter-add | solution.py:36
  145.5 3.3 %gather_fusion.1 = bf16[32,128,256]{2,1,0:T(8,128)(2,1)} fusion(bf16[16,128,256]{2,1,0:T(8,128)(2,1)} %get-tuple-element.189, s32[1024]{0:T(1024)S(1)} %pad_clamp_fusion.6), kind=kCustom, calls=%fused_computation.1.clone.1 | custom fusion | bytes 4194432 | tf_op jit(solution)/shard_map/while/body/eval_jaxpr/gather | solution.py:22
  148.7 3.0 %gather_fusion = bf16[32,128,256]{2,1,0:T(8,128)(2,1)} fusion(bf16[8,128,256]{2,1,0:T(8,128)(2,1)} %get-tuple-element.187, s32[1024]{0:T(1024)S(1)} %pad_clamp_fusion.5), kind=kCustom, calls=%fused_computation.clone.1 | custom fusion | bytes 4194432 | tf_op jit(solution)/shard_map/while/body/eval_jaxpr/gather | solution.py:21
  151.8 3.4 %fusion.43 = bf16[32,128,128]{2,1,0:T(8,128)(2,1)S(1)} fusion(bf16[32,128,256]{2,1,0:T(8,128)(2,1)} %gather_fusion, bf16[32,128,256]{2,1,0:T(8,128)(2,1)} %gather_fusion.1, bf16[4,32,128,128]{3,2,1,0:T(8,128)(2,1)} %get-tuple-element.186, s32[]{:T(128)S(6)} %copy.44), kind=kOutput, calls=%fused_computation.11.clone.1 | convolution fusion | flops 273154048 | bytes 6291460 | tf_op jit(solution)/shard_map/while/body/eval_jaxpr/gur,gir->gui/dot_general | solution.py:23
  155.2 1.0 copy-done.3
  156.2 2.7 %fusion.45 = f32[32,128,256]{2,1,0:T(8,128)} fusion(bf16[32,128,128]{2,1,0:T(8,128)(2,1)S(1)} %fusion.43, bf16[32,128,256]{2,1,0:T(8,128)(2,1)S(1)} %copy-done.1), kind=kOutput, calls=%fused_computation.75.clone.1 | convolution fusion | flops 268435456 | bytes 7340032 | tf_op jit(solution)/shard_map/while/body/eval_jaxpr/gui,gur->gir/dot_general | solution.py:33
  158.9 6.5 %scatter_fusion.1 = f32[16,128,256]{2,1,0:T(8,128)S(1)} fusion(f32[16,128,256]{2,1,0:T(8,128)S(1)} %get-tuple-element.175, s32[32]{0:T(128)S(1)} %get-tuple-element.163, f32[32,128,256]{2,1,0:T(8,128)} %fusion.45), kind=kCustom, calls=%fused_computation.4.clone.1 | custom fusion | flops 1048576 | bytes 12583040 | tf_op jit(solution)/shard_map/while/body/eval_jaxpr/scatter-add | solution.py:37
  165.4 4.6 %fusion.44 = f32[32,128,256]{2,1,0:T(8,128)} fusion(bf16[32,128,128]{2,1,0:T(8,128)(2,1)} %copy-done.3, bf16[32,128,256]{2,1,0:T(8,128)(2,1)} %gather_fusion.1), kind=kOutput, calls=%fused_computation.74.clone.1 | convolution fusion | flops 268435456 | bytes 7340032 | tf_op jit(solution)/shard_map/while/body/eval_jaxpr/gui,gir->gur/dot_general | solution.py:30
  169.9 6.5 %scatter_fusion = f32[8,128,256]{2,1,0:T(8,128)S(1)} fusion(f32[8,128,256]{2,1,0:T(8,128)S(1)} %get-tuple-element.174, s32[32]{0:T(128)S(1)} %get-tuple-element.162, f32[32,128,256]{2,1,0:T(8,128)} %fusion.44), kind=kCustom, calls=%fused_computation.3.clone.1 | custom fusion | flops 1048576 | bytes 12583040 | tf_op jit(solution)/shard_map/while/body/eval_jaxpr/scatter-add | solution.py:36
  176.4 3.3 %gather_fusion.1 = bf16[32,128,256]{2,1,0:T(8,128)(2,1)} fusion(bf16[16,128,256]{2,1,0:T(8,128)(2,1)} %get-tuple-element.189, s32[1024]{0:T(1024)S(1)} %pad_clamp_fusion.6), kind=kCustom, calls=%fused_computation.1.clone.1 | custom fusion | bytes 4194432 | tf_op jit(solution)/shard_map/while/body/eval_jaxpr/gather | solution.py:22
  179.7 3.0 %gather_fusion = bf16[32,128,256]{2,1,0:T(8,128)(2,1)} fusion(bf16[8,128,256]{2,1,0:T(8,128)(2,1)} %get-tuple-element.187, s32[1024]{0:T(1024)S(1)} %pad_clamp_fusion.5), kind=kCustom, calls=%fused_computation.clone.1 | custom fusion | bytes 4194432 | tf_op jit(solution)/shard_map/while/body/eval_jaxpr/gather | solution.py:21
  182.8 3.4 %fusion.43 = bf16[32,128,128]{2,1,0:T(8,128)(2,1)S(1)} fusion(bf16[32,128,256]{2,1,0:T(8,128)(2,1)} %gather_fusion, bf16[32,128,256]{2,1,0:T(8,128)(2,1)} %gather_fusion.1, bf16[4,32,128,128]{3,2,1,0:T(8,128)(2,1)} %get-tuple-element.186, s32[]{:T(128)S(6)} %copy.44), kind=kOutput, calls=%fused_computation.11.clone.1 | convolution fusion | flops 273154048 | bytes 6291460 | tf_op jit(solution)/shard_map/while/body/eval_jaxpr/gur,gir->gui/dot_general | solution.py:23
  186.2 1.0 copy-done.3
  187.2 2.7 %fusion.45 = f32[32,128,256]{2,1,0:T(8,128)} fusion(bf16[32,128,128]{2,1,0:T(8,128)(2,1)S(1)} %fusion.43, bf16[32,128,256]{2,1,0:T(8,128)(2,1)S(1)} %copy-done.1), kind=kOutput, calls=%fused_computation.75.clone.1 | convolution fusion | flops 268435456 | bytes 7340032 | tf_op jit(solution)/shard_map/while/body/eval_jaxpr/gui,gur->gir/dot_general | solution.py:33
  189.9 6.5 %scatter_fusion.1 = f32[16,128,256]{2,1,0:T(8,128)S(1)} fusion(f32[16,128,256]{2,1,0:T(8,128)S(1)} %get-tuple-element.175, s32[32]{0:T(128)S(1)} %get-tuple-element.163, f32[32,128,256]{2,1,0:T(8,128)} %fusion.45), kind=kCustom, calls=%fused_computation.4.clone.1 | custom fusion | flops 1048576 | bytes 12583040 | tf_op jit(solution)/shard_map/while/body/eval_jaxpr/scatter-add | solution.py:37
  196.3 4.6 %fusion.44 = f32[32,128,256]{2,1,0:T(8,128)} fusion(bf16[32,128,128]{2,1,0:T(8,128)(2,1)} %copy-done.3, bf16[32,128,256]{2,1,0:T(8,128)(2,1)} %gather_fusion.1), kind=kOutput, calls=%fused_computation.74.clone.1 | convolution fusion | flops 268435456 | bytes 7340032 | tf_op jit(solution)/shard_map/while/body/eval_jaxpr/gui,gir->gur/dot_general | solution.py:30
  200.9 6.5 %scatter_fusion = f32[8,128,256]{2,1,0:T(8,128)S(1)} fusion(f32[8,128,256]{2,1,0:T(8,128)S(1)} %get-tuple-element.174, s32[32]{0:T(128)S(1)} %get-tuple-element.162, f32[32,128,256]{2,1,0:T(8,128)} %fusion.44), kind=kCustom, calls=%fused_computation.3.clone.1 | custom fusion | flops 1048576 | bytes 12583040 | tf_op jit(solution)/shard_map/while/body/eval_jaxpr/scatter-add | solution.py:36
  207.5 24.1 %all_to_all.5 = bf16[16,128,256]{2,1,0:T(8,128)(2,1)S(1)} all-to-all(bf16[16,128,256]{2,1,0:T(8,128)(2,1)S(1)} %convert_element_type.21), channel_id=1, replica_groups=mesh['users'=16,'rep'=2] {'users'}, dimensions={0} | all-to-all | bytes 2097152 | tf_op jit(solution)/shard_map/all_to_all | solution.py:89
  231.6 0.7 fusion.9
  232.3 0.7 copy.19
  233.1 18.4 %all-reduce.3.cloned.1.call-done = (f32[1024,256]{1,0:T(8,128)}, f32[256,256]{1,0:T(8,128)}) async-done(((f32[1024,256]{1,0:T(8,128)}, f32[256,256]{1,0:T(8,128)}), (f32[1024,256]{1,0:T(8,128)}, f32[256,256]{1,0:T(8,128)})) %all-reduce.3.cloned.1.call-update) | async-done | bytes 1310736 | tf_op jit(solution)/shard_map/psum | solution.py:97
  251.5 1.8 multiply_subtract_fusion.1
  253.3 2.7 %multiply_subtract_fusion = (f32[1024,256]{1,0:T(8,128)}, f32[1024,256]{1,0:T(8,128)}) fusion(f32[1024,256]{1,0:T(8,128)S(1)} %copy-done.5, f32[1024,256]{1,0:T(8,128)} %get-tuple-element.87, f32[1024,256]{1,0:T(8,128)S(1)} %copy-done.6), kind=kLoop, calls=%fused_computation.25 | loop fusion | flops 1048576 | bytes 5242880 | tf_op jit(solution)/shard_map/sub | solution.py:56
  (90 shorter events, 5.1 us)
Async XLA Ops:
  7.2 244.3 %all-reduce.3.cloned.1.call-start = ((), (), s32[]{:S(2)}) async-start(), calls=%async_computation.1 | async-start | bytes 2621440 | tf_op jit(solution)/shard_map/psum | solution.py:97
  9.6 14.0 %copy-start.14 = (s32[1,1,128]{2,1,0:T(1,128)S(1)}, s32[1,1,128]{2,1,0:T(1,128)}, u32[]{:S(2)}) copy-start(s32[1,1,128]{2,1,0:T(1,128)} %param.16) | copy-start | bytes 1540
  9.6 14.6 %copy-start.15 = (s32[1,1,128]{2,1,0:T(1,128)S(1)}, s32[1,1,128]{2,1,0:T(1,128)}, u32[]{:S(2)}) copy-start(s32[1,1,128]{2,1,0:T(1,128)} %param.15) | copy-start | bytes 1540
  9.7 15.3 %copy-start.4 = (f32[1024,256]{1,0:T(8,128)S(1)}, f32[1024,256]{1,0:T(8,128)}, u32[]{:S(2)}) copy-start(f32[1024,256]{1,0:T(8,128)} %param.10) | copy-start | bytes 3145732
  10.6 35.6 %copy-start.12 = (bf16[1,128,256]{2,1,0:T(8,128)(2,1)S(1)}, bf16[1,128,256]{2,1,0:T(8,128)(2,1)}, u32[]{:S(2)}) copy-start(bf16[1,128,256]{2,1,0:T(8,128)(2,1)} %get-tuple-element.104) | copy-start | bytes 196612
  10.6 40.7 %copy-start.11 = (bf16[1,128,256]{2,1,0:T(8,128)(2,1)S(1)}, bf16[1,128,256]{2,1,0:T(8,128)(2,1)}, u32[]{:S(2)}) copy-start(bf16[1,128,256]{2,1,0:T(8,128)(2,1)} %get-tuple-element.103) | copy-start | bytes 196612
  10.6 46.8 %copy-start.10 = (bf16[1,128,256]{2,1,0:T(8,128)(2,1)S(1)}, bf16[1,128,256]{2,1,0:T(8,128)(2,1)}, u32[]{:S(2)}) copy-start(bf16[1,128,256]{2,1,0:T(8,128)(2,1)} %get-tuple-element.102) | copy-start | bytes 196612
  10.6 52.0 %copy-start.9 = (bf16[1,128,256]{2,1,0:T(8,128)(2,1)S(1)}, bf16[1,128,256]{2,1,0:T(8,128)(2,1)}, u32[]{:S(2)}) copy-start(bf16[1,128,256]{2,1,0:T(8,128)(2,1)} %get-tuple-element.101) | copy-start | bytes 196612
  10.7 71.5 %collective-permute-start.14 = (bf16[1,128,256]{2,1,0:T(8,128)(2,1)S(1)}, bf16[1,128,256]{2,1,0:T(8,128)(2,1)S(1)}, u32[]{:S(2)}, u32[]{:S(2)}) collective-permute-start(bf16[1,128,256]{2,1,0:T(8,128)(2,1)S(1)} %get-tuple-element.95), channel_id=1, source_target_pairs={{0,30},{2,28},{4,26},{6,24},{8,22},{10,20},{12,18},{14,16},{16,14}... | collective-permute-start | bytes 196616 | tf_op jit(solution)/shard_map/ppermute | solution.py:84
  17.7 64.5 %collective-permute-start.13 = (bf16[1,128,256]{2,1,0:T(8,128)(2,1)S(1)}, bf16[1,128,256]{2,1,0:T(8,128)(2,1)S(1)}, u32[]{:S(2)}, u32[]{:S(2)}) collective-permute-start(bf16[1,128,256]{2,1,0:T(8,128)(2,1)S(1)} %get-tuple-element.96), channel_id=1, source_target_pairs={{0,28},{2,30},{4,24},{6,26},{8,20},{10,22},{12,16},{14,18},{16,12}... | collective-permute-start | bytes 196616 | tf_op jit(solution)/shard_map/ppermute | solution.py:84
  17.8 64.3 %collective-permute-start.12 = (bf16[1,128,256]{2,1,0:T(8,128)(2,1)S(1)}, bf16[1,128,256]{2,1,0:T(8,128)(2,1)S(1)}, u32[]{:S(2)}, u32[]{:S(2)}) collective-permute-start(bf16[1,128,256]{2,1,0:T(8,128)(2,1)S(1)} %get-tuple-element.97), channel_id=1, source_target_pairs={{0,26},{2,24},{4,30},{6,28},{8,18},{10,16},{12,22},{14,20},{16,10}... | collective-permute-start | bytes 196616 | tf_op jit(solution)/shard_map/ppermute | solution.py:84
  21.4 60.7 %collective-permute-start.11 = (bf16[1,128,256]{2,1,0:T(8,128)(2,1)S(1)}, bf16[1,128,256]{2,1,0:T(8,128)(2,1)S(1)}, u32[]{:S(2)}, u32[]{:S(2)}) collective-permute-start(bf16[1,128,256]{2,1,0:T(8,128)(2,1)S(1)} %get-tuple-element.98), channel_id=1, source_target_pairs={{0,24},{2,26},{4,28},{6,30},{8,16},{10,18},{12,20},{14,22},{16,8},... | collective-permute-start | bytes 196616 | tf_op jit(solution)/shard_map/ppermute | solution.py:84
  21.6 4.5 %collective-permute-start = (bf16[1,128,256]{2,1,0:T(8,128)(2,1)}, bf16[1,128,256]{2,1,0:T(8,128)(2,1)S(1)}, u32[]{:S(2)}, u32[]{:S(2)}) collective-permute-start(bf16[1,128,256]{2,1,0:T(8,128)(2,1)} %get-tuple-element.109), channel_id=1, source_target_pairs={{0,2},{2,0},{4,6},{6,4},{8,10},{10,8},{12,14},{14,12},{16,18},{18,... | collective-permute-start | bytes 196616 | tf_op jit(solution)/shard_map/ppermute | solution.py:84
  26.1 4.5 %collective-permute-start.1 = (bf16[1,128,256]{2,1,0:T(8,128)(2,1)}, bf16[1,128,256]{2,1,0:T(8,128)(2,1)S(1)}, u32[]{:S(2)}, u32[]{:S(2)}) collective-permute-start(bf16[1,128,256]{2,1,0:T(8,128)(2,1)} %get-tuple-element.108), channel_id=1, source_target_pairs={{0,4},{2,6},{4,0},{6,2},{8,12},{10,14},{12,8},{14,10},{16,20},{18,... | collective-permute-start | bytes 196616 | tf_op jit(solution)/shard_map/ppermute | solution.py:84
  30.5 5.4 %collective-permute-start.2 = (bf16[1,128,256]{2,1,0:T(8,128)(2,1)}, bf16[1,128,256]{2,1,0:T(8,128)(2,1)S(1)}, u32[]{:S(2)}, u32[]{:S(2)}) collective-permute-start(bf16[1,128,256]{2,1,0:T(8,128)(2,1)} %get-tuple-element.107), channel_id=1, source_target_pairs={{0,6},{2,4},{4,2},{6,0},{8,14},{10,12},{12,10},{14,8},{16,22},{18,... | collective-permute-start | bytes 196616 | tf_op jit(solution)/shard_map/ppermute | solution.py:84
  35.9 4.9 %collective-permute-start.3 = (bf16[1,128,256]{2,1,0:T(8,128)(2,1)}, bf16[1,128,256]{2,1,0:T(8,128)(2,1)S(1)}, u32[]{:S(2)}, u32[]{:S(2)}) collective-permute-start(bf16[1,128,256]{2,1,0:T(8,128)(2,1)} %get-tuple-element.106), channel_id=1, source_target_pairs={{0,8},{2,10},{4,12},{6,14},{8,0},{10,2},{12,4},{14,6},{16,24},{18,... | collective-permute-start | bytes 196616 | tf_op jit(solution)/shard_map/ppermute | solution.py:84
  40.8 5.4 %collective-permute-start.4 = (bf16[1,128,256]{2,1,0:T(8,128)(2,1)}, bf16[1,128,256]{2,1,0:T(8,128)(2,1)S(1)}, u32[]{:S(2)}, u32[]{:S(2)}) collective-permute-start(bf16[1,128,256]{2,1,0:T(8,128)(2,1)} %get-tuple-element.105), channel_id=1, source_target_pairs={{0,10},{2,8},{4,14},{6,12},{8,2},{10,0},{12,6},{14,4},{16,26},{18,... | collective-permute-start | bytes 196616 | tf_op jit(solution)/shard_map/ppermute | solution.py:84
  46.2 5.2 %collective-permute-start.5 = (bf16[1,128,256]{2,1,0:T(8,128)(2,1)S(1)}, bf16[1,128,256]{2,1,0:T(8,128)(2,1)S(1)}, u32[]{:S(2)}, u32[]{:S(2)}) collective-permute-start(bf16[1,128,256]{2,1,0:T(8,128)(2,1)S(1)} %copy-done.12), channel_id=1, source_target_pairs={{0,12},{2,14},{4,8},{6,10},{8,4},{10,6},{12,0},{14,2},{16,28},{18,... | collective-permute-start | bytes 196616 | tf_op jit(solution)/shard_map/ppermute | solution.py:84
  51.4 6.1 %collective-permute-start.6 = (bf16[1,128,256]{2,1,0:T(8,128)(2,1)S(1)}, bf16[1,128,256]{2,1,0:T(8,128)(2,1)S(1)}, u32[]{:S(2)}, u32[]{:S(2)}) collective-permute-start(bf16[1,128,256]{2,1,0:T(8,128)(2,1)S(1)} %copy-done.11), channel_id=1, source_target_pairs={{0,14},{2,12},{4,10},{6,8},{8,6},{10,4},{12,2},{14,0},{16,30},{18,... | collective-permute-start | bytes 196616 | tf_op jit(solution)/shard_map/ppermute | solution.py:84
  57.4 5.2 %collective-permute-start.7 = (bf16[1,128,256]{2,1,0:T(8,128)(2,1)S(1)}, bf16[1,128,256]{2,1,0:T(8,128)(2,1)S(1)}, u32[]{:S(2)}, u32[]{:S(2)}) collective-permute-start(bf16[1,128,256]{2,1,0:T(8,128)(2,1)S(1)} %copy-done.10), channel_id=1, source_target_pairs={{0,16},{2,18},{4,20},{6,22},{8,24},{10,26},{12,28},{14,30},{16,0},... | collective-permute-start | bytes 196616 | tf_op jit(solution)/shard_map/ppermute | solution.py:84
  62.6 6.1 %collective-permute-start.8 = (bf16[1,128,256]{2,1,0:T(8,128)(2,1)S(1)}, bf16[1,128,256]{2,1,0:T(8,128)(2,1)S(1)}, u32[]{:S(2)}, u32[]{:S(2)}) collective-permute-start(bf16[1,128,256]{2,1,0:T(8,128)(2,1)S(1)} %copy-done.9), channel_id=1, source_target_pairs={{0,18},{2,16},{4,22},{6,20},{8,26},{10,24},{12,30},{14,28},{16,2},... | collective-permute-start | bytes 196616 | tf_op jit(solution)/shard_map/ppermute | solution.py:84
  68.7 6.4 %collective-permute-start.9 = (bf16[1,128,256]{2,1,0:T(8,128)(2,1)S(1)}, bf16[1,128,256]{2,1,0:T(8,128)(2,1)S(1)}, u32[]{:S(2)}, u32[]{:S(2)}) collective-permute-start(bf16[1,128,256]{2,1,0:T(8,128)(2,1)S(1)} %get-tuple-element.100), channel_id=1, source_target_pairs={{0,20},{2,22},{4,16},{6,18},{8,28},{10,30},{12,24},{14,26},{16,4},... | collective-permute-start | bytes 196616 | tf_op jit(solution)/shard_map/ppermute | solution.py:84
  75.1 7.0 %collective-permute-start.10 = (bf16[1,128,256]{2,1,0:T(8,128)(2,1)S(1)}, bf16[1,128,256]{2,1,0:T(8,128)(2,1)S(1)}, u32[]{:S(2)}, u32[]{:S(2)}) collective-permute-start(bf16[1,128,256]{2,1,0:T(8,128)(2,1)S(1)} %get-tuple-element.99), channel_id=1, source_target_pairs={{0,22},{2,20},{4,18},{6,16},{8,30},{10,28},{12,26},{14,24},{16,6},... | collective-permute-start | bytes 196616 | tf_op jit(solution)/shard_map/ppermute | solution.py:84
  82.2 1.0 copy-start.2
  89.8 4.4 %copy-start.1 = (bf16[32,128,256]{2,1,0:T(8,128)(2,1)S(1)}, bf16[32,128,256]{2,1,0:T(8,128)(2,1)}, u32[]{:S(2)}) copy-start(bf16[32,128,256]{2,1,0:T(8,128)(2,1)} %gather_fusion) | copy-start | bytes 6291460 | tf_op jit(solution)/shard_map/while
  93.3 1.0 copy-start.3
  120.8 4.4 %copy-start.1 = (bf16[32,128,256]{2,1,0:T(8,128)(2,1)S(1)}, bf16[32,128,256]{2,1,0:T(8,128)(2,1)}, u32[]{:S(2)}) copy-start(bf16[32,128,256]{2,1,0:T(8,128)(2,1)} %gather_fusion) | copy-start | bytes 6291460 | tf_op jit(solution)/shard_map/while
  124.2 1.0 copy-start.3
  151.8 4.4 %copy-start.1 = (bf16[32,128,256]{2,1,0:T(8,128)(2,1)S(1)}, bf16[32,128,256]{2,1,0:T(8,128)(2,1)}, u32[]{:S(2)}) copy-start(bf16[32,128,256]{2,1,0:T(8,128)(2,1)} %gather_fusion) | copy-start | bytes 6291460 | tf_op jit(solution)/shard_map/while
  155.2 1.0 copy-start.3
  182.8 4.4 %copy-start.1 = (bf16[32,128,256]{2,1,0:T(8,128)(2,1)S(1)}, bf16[32,128,256]{2,1,0:T(8,128)(2,1)}, u32[]{:S(2)}) copy-start(bf16[32,128,256]{2,1,0:T(8,128)(2,1)} %gather_fusion) | copy-start | bytes 6291460 | tf_op jit(solution)/shard_map/while
  186.2 1.0 copy-start.3
  207.4 24.2 %copy-start = (f32[8,128,256]{2,1,0:T(8,128)}, f32[8,128,256]{2,1,0:T(8,128)S(1)}, u32[]{:S(2)}) copy-start(f32[8,128,256]{2,1,0:T(8,128)S(1)} %get-tuple-element.69) | copy-start | bytes 3145732
  207.4 24.2 %copy-start.13 = (s32[1,1,16]{2,1,0:T(1,128)S(1)}, s32[1,1,16]{2,1,0:T(1,128)}, u32[]{:S(2)}) copy-start(s32[1,1,16]{2,1,0:T(1,128)} %param.17) | copy-start | bytes 196
  231.6 19.9 %copy-start.7 = (f32[256,256]{1,0:T(8,128)S(1)}, f32[256,256]{1,0:T(8,128)}, u32[]{:S(2)}) copy-start(f32[256,256]{1,0:T(8,128)} %param.12) | copy-start | bytes 786436
  231.6 19.9 %copy-start.8 = (f32[256,256]{1,0:T(8,128)S(1)}, f32[256,256]{1,0:T(8,128)}, u32[]{:S(2)}) copy-start(f32[256,256]{1,0:T(8,128)} %param.13) | copy-start | bytes 786436
  231.6 21.7 %copy-start.5 = (f32[1024,256]{1,0:T(8,128)S(1)}, f32[1024,256]{1,0:T(8,128)}, u32[]{:S(2)}) copy-start(f32[1024,256]{1,0:T(8,128)} %param.10) | copy-start | bytes 3145732
  231.6 21.6 %copy-start.6 = (f32[1024,256]{1,0:T(8,128)S(1)}, f32[1024,256]{1,0:T(8,128)}, u32[]{:S(2)}) copy-start(f32[1024,256]{1,0:T(8,128)} %param.11) | copy-start | bytes 3145732
Sparse Core Ops, SparseCore 0:
  233.2 18.2 all-reduce.2
